TPU v7x, 32 devices: a whole 2x2x4 slice. The times are simulated.
32 devices in a mesh: row: 16 (over z, x, core), col: 2 (over y).
Axes of the slice: x: 2, y: 2, z: 4, core: 2. Of those that a mesh axis runs over, the one named last changes fastest.
Arguments:
- base_velocity: bfloat16 [3, 512, 256, 384], P(None, 'row', 'col'), may hold values from -6 to 6
- velocity_step: bfloat16 [3, 512, 256, 384], P(None, 'row', 'col'), may hold values from -6 to 6
- adjoint_velocity: bfloat16 [3, 512, 256, 384], P(None, 'row', 'col'), may hold values from -6 to 6
- increment_weight: float32 [1], replicated, may hold values from 0.3 to 0.9
- streamwise_first: bfloat16 [3, 128, 128], replicated, may hold values from -0.3125 to 0.3125
- streamwise_second: bfloat16 [3, 128, 128], replicated, may hold values from -0.3125 to 0.3125
- normal_first: bfloat16 [512, 512], replicated, may hold values from -0.25 to 0.25
- normal_second: bfloat16 [512, 512], replicated, may hold values from -0.25 to 0.25
- spanwise_first: bfloat16 [256, 256], replicated, may hold values from -0.375 to 0.375
- spanwise_second: bfloat16 [256, 256], replicated, may hold values from -0.375 to 0.375
- wall_profile: float32 [2, 512], P(None, 'row'), may hold values from 0.5 to 1.5
Outputs:
- adjoint_tendency: bfloat16 [3, 512, 256, 384], P(None, 'row', 'col')
All inputs are finite; a program needn't handle non-finite values.
Results may differ from a plain program's by a relative error of at most 0.012.
Values may be sent and summed in bfloat16 or wider, within the bound.
No kernel may reach another device: no remote copies, remote signals or barrier semaphores. Data moves between devices by JAX's collectives and lax.ppermute only.
A program may use at most 448 MiB of HBM per device.

v0:
```python
import jax
import jax.numpy as jnp
from jax import lax
from jax.sharding import PartitionSpec as P


def along_stream(field, operators):
    block_width = operators[0].shape[1]
    block_count = field.shape[-1] // block_width
    tiles = field.reshape(field.shape[:-1] + (block_count, block_width))
    joined = jnp.concatenate([blocks[k] for blocks in operators for k in range(3)], axis=1)
    product = jnp.dot(tiles, joined, preferred_element_type=jnp.float32)
    results = []
    for number in range(len(operators)):
        start = 3 * number * block_width
        lower = product[..., start : start + block_width]
        middle = product[..., start + block_width : start + 2 * block_width]
        upper = product[..., start + 2 * block_width : start + 3 * block_width]
        combined = jnp.roll(lower, 1, axis=-2) + middle + jnp.roll(upper, -1, axis=-2)
        results.append(combined.reshape(field.shape))
    return results


def normal_products(speed, adjoint, first_op, second_op):
    slope_speed = jnp.einsum("wy,cyp->cwp", first_op, speed, preferred_element_type=jnp.float32)
    stacked = jnp.concatenate([first_op, second_op], axis=0)
    both = jnp.einsum("wy,cyp->cwp", stacked, adjoint, preferred_element_type=jnp.float32)
    lines = first_op.shape[0]
    return (slope_speed, both[:, :lines], both[:, lines:])


def span_products(speed, adjoint, first_op, second_op):
    slope_speed = jnp.einsum("vz,cyzx->cyvx", first_op, speed, preferred_element_type=jnp.float32)
    stacked = jnp.concatenate([first_op, second_op], axis=0)
    both = jnp.einsum("vz,cyzx->cyvx", stacked, adjoint, preferred_element_type=jnp.float32)
    planes = first_op.shape[0]
    return (slope_speed, both[:, :, :planes], both[:, :, planes:])


def component_mask(which, ndim):
    return (jnp.arange(3) == which).astype(jnp.float32).reshape((3,) + (1,) * (ndim - 1))


def adjoint_terms(velocity, adjoint, slope_velocity, slope_adjoint, curve_adjoint, direction):
    cross = jnp.sum(adjoint.astype(jnp.float32) * slope_velocity, axis=0)
    advect = velocity[direction].astype(jnp.float32)[None] * slope_adjoint
    return curve_adjoint - advect + component_mask(direction, adjoint.ndim) * cross[None]


def per_device(
    base_velocity,
    velocity_step,
    adjoint_velocity,
    increment_weight,
    streamwise_first,
    streamwise_second,
    normal_first,
    normal_second,
    spanwise_first,
    spanwise_second,
    wall_profile,
):
    velocity = (
        base_velocity.astype(jnp.float32) + increment_weight[0] * velocity_step.astype(jnp.float32)
    ).astype(jnp.bfloat16)
    (slope_speed,) = along_stream(velocity, [streamwise_first])
    slope_adjoint, curve_adjoint = along_stream(
        adjoint_velocity, [streamwise_first, streamwise_second]
    )
    near = adjoint_terms(velocity, adjoint_velocity, slope_speed, slope_adjoint, curve_adjoint, 0)
    local_rows = velocity.shape[1]
    local_planes = velocity.shape[2]
    stream_cells = velocity.shape[3]
    flat_speed = velocity.reshape(3, local_rows, local_planes * stream_cells)
    flat_adjoint = adjoint_velocity.reshape(3, local_rows, local_planes * stream_cells)
    speed_lines, adjoint_lines = (
        lax.all_to_all(flat_speed, "row", split_axis=2, concat_axis=1, tiled=True),
        lax.all_to_all(flat_adjoint, "row", split_axis=2, concat_axis=1, tiled=True),
    )
    normal_speed, normal_adjoint, normal_curve = normal_products(
        speed_lines, adjoint_lines, normal_first, normal_second
    )
    normal_term = adjoint_terms(
        speed_lines, adjoint_lines, normal_speed, normal_adjoint, normal_curve, 1
    ).astype(jnp.bfloat16)
    strip = jnp.stack([normal_speed[0, 0], normal_speed[0, -1]]).astype(jnp.bfloat16)
    wall_shear = lax.all_gather(strip, "row", axis=1, tiled=True).reshape(
        2, local_planes, stream_cells
    )
    normal_home = lax.all_to_all(
        normal_term, "row", split_axis=1, concat_axis=2, tiled=True
    ).reshape(3, local_rows, local_planes, stream_cells)
    speed_span, adjoint_span = (
        lax.all_to_all(velocity, "col", split_axis=1, concat_axis=2, tiled=True),
        lax.all_to_all(adjoint_velocity, "col", split_axis=1, concat_axis=2, tiled=True),
    )
    span_speed, span_adjoint, span_curve = span_products(
        speed_span, adjoint_span, spanwise_first, spanwise_second
    )
    span_term = adjoint_terms(
        speed_span, adjoint_span, span_speed, span_adjoint, span_curve, 2
    ).astype(jnp.bfloat16)
    span_home = lax.all_to_all(span_term, "col", split_axis=2, concat_axis=1, tiled=True)
    far_terms = (normal_home.astype(jnp.float32) + span_home.astype(jnp.float32)).astype(
        jnp.bfloat16
    )
    (shear_slope,) = along_stream(wall_shear, [streamwise_first])
    forcing = (
        wall_profile[0][:, None, None] * shear_slope[0][None]
        + wall_profile[1][:, None, None] * shear_slope[1][None]
    )
    total = near + far_terms.astype(jnp.float32) + component_mask(0, 4) * forcing[None]
    return total.astype(jnp.bfloat16)


def solution(mesh):
    placed = (
        P(None, "row", "col", None),
        P(None, "row", "col", None),
        P(None, "row", "col", None),
        P(),
        P(),
        P(),
        P(),
        P(),
        P(),
        P(),
        P(None, "row"),
    )
    return jax.shard_map(
        per_device,
        mesh=mesh,
        in_specs=placed,
        out_specs=P(None, "row", "col", None),
        check_vma=False,
    )
```

profile of v0, /device:TPU:13, one launch (start us, length us, event | category | flops | bytes accessed | tf_op | source)
XLA Modules:
  0.0 1365.6 jit_solution(14723358383659704467)
XLA Ops:
  0.0 9.1 copy.205
  16.6 12.6 copy.186
  29.2 12.6 copy.185
  42.5 12.5 add_convert_fusion.2
  55.0 8.5 copy.207
  63.5 55.0 %all-to-all-done.3 = bf16[3,32,128,384]{3,2,0,1:T(8,128)(2,1)} async-done(((bf16[3,32,128,384]{3,2,0,1:T(8,128)(2,1)}), bf16[3,32,128,384]{3,2,0,1:T(8,128)(2,1)}, u32[]{:S(2)}, u32[]{:S(2)}) %all-to-all-start.3) | async-done | bytes 9437216 | tf_op jit(solution)/shard_map/all_to_all | solution.py:95
  118.5 8.5 all-to-all-start.4
  127.0 81.2 %copy.232 = bf16[3,32,128,384]{1,0,3,2:T(4,128)(2,1)} copy(bf16[3,32,128,384]{2,3,1,0:T(8,128)(2,1)} %add_convert_fusion.2) | data formatting | bytes 18874368 | tf_op jit(solution)/shard_map/reshape | solution.py:74
  208.2 36.1 %reshape.104 = bf16[16,2,147456]{2,1,0:T(2,128)(2,1)} reshape(bf16[49152,3,32]{2,1,0:T(4,128)(2,1)} %bitcast.130) | data formatting | bytes 18874368
  252.0 48.7 %copy.195 = bf16[3,32,128,384]{1,0,3,2:T(4,128)(2,1)} copy(bf16[3,32,128,384]{3,2,1,0:T(8,128)(2,1)} %param.13) | data formatting | bytes 18874368 | tf_op args[2]
  300.7 36.1 %reshape.102 = bf16[16,2,147456]{2,1,0:T(2,128)(2,1)} reshape(bf16[49152,3,32]{2,1,0:T(4,128)(2,1)} %bitcast.131) | data formatting | bytes 18874368
  336.8 117.9 %all-to-all-done.1 = bf16[16,2,147456]{2,1,0:T(2,128)(2,1)} async-done(((bf16[16,2,147456]{2,1,0:T(2,128)(2,1)}), bf16[16,2,147456]{2,1,0:T(2,128)(2,1)}, u32[]{:S(2)}, u32[]{:S(2)}) %all-to-all-start.1) | async-done | bytes 9437216 | tf_op jit(solution)/shard_map/all_to_all | solution.py:77
  462.4 12.7 copy.183
  476.4 40.9 %convolution_bitcast_fusion = f32[3,32,128,3,768]{2,4,3,1,0:T(8,128)} fusion(bf16[3,32,128,3,128]{2,4,3,1,0:T(8,128)(2,1)} %bitcast.132, bf16[128,768]{0,1:T(8,128)(2,1)S(1)} %bitcast_dynamic-update-slice_fusion), kind=kOutput, calls=%fused_computation | convolution fusion | flops 7247757312 | bytes 122880000 | tf_op jit(solution)/shard_map/dot_general | solution.py:12
  517.3 31.5 %fusion.31 = (f32[3,32,128,2,128]{2,4,3,1,0:T(8,128)}, f32[3,32,128,2,128]{2,4,3,1,0:T(8,128)}, f32[3,32,128,2,128]{2,4,3,1,0:T(8,128)}, f32[3,32,128,2,128]{2,4,3,1,0:T(8,128)}) fusion(f32[3,32,128,3,768]{2,4,3,1,0:T(8,128)} %convolution_bitcast_fusion), kind=kLoop, calls=%fused_computation.69 | loop fusion | bytes 100663296 | tf_op jit(solution)/shard_map/jit(_roll_static)/slice | solution.py:19
  548.9 9.1 copy.206
  558.0 12.6 copy.209
  576.3 12.7 fusion.9
  589.1 18.7 %convolution_bitcast_fusion.2 = f32[3,16,512,384]{3,2,1,0:T(8,128)} fusion(bf16[3,16,256,384]{3,2,1,0:T(8,128)(2,1)} %bitcast.134, bf16[256,256]{1,0:T(8,128)(2,1)S(1)} %copy-done.8, bf16[256,256]{1,0:T(8,128)(2,1)S(1)} %copy-done.1), kind=kOutput, calls=%fused_computation.28 | convolution fusion | flops 4832362496 | bytes 47448064 | tf_op jit(solution)/shard_map/vz,cyzx->cyvx/dot_general | solution.py:35
  607.8 19.0 %fusion.2 = bf16[3,16,256,384]{3,2,1,0:T(8,128)(2,1)} fusion(f32[3,16,512,384]{3,2,1,0:T(8,128)} %convolution_bitcast_fusion.2, f32[16,256,384]{2,1,0:T(8,128)} %fusion.9, f32[3]{0:T(128)S(1)} %compare_convert_fusion, f32[16,256,384]{2,1,0:T(8,128)S(1)} %bitcast.146), kind=kLoop, calls=%fused_computation.5 | loop fusion | flops 23592960 | bytes 59768844 | tf_op jit(solution)/shard_map/convert_element_type | solution.py:102
  626.7 12.8 copy.212
  639.6 35.8 %reshape.105 = bf16[49152,3,32]{2,1,0:T(4,128)(2,1)} reshape(bf16[16,2,147456]{2,1,0:T(2,128)(2,1)} %all-to-all-done.1) | data formatting | bytes 18874368
  675.4 58.5 %copy.234 = bf16[3,32,16,3072]{3,1,2,0:T(8,128)(2,1)} copy(bf16[3,32,16,3072]{1,0,3,2:T(4,128)(2,1)} %bitcast.126) | data formatting | bytes 18874368 | tf_op jit(solution)/shard_map/all_to_all | solution.py:77
  733.9 47.1 %copy.233 = bf16[3,32,16,3072]{3,2,1,0:T(8,128)(2,1)} copy(bf16[3,32,16,3072]{1,0,3,2:T(4,128)(2,1)} %bitcast.127) | data formatting | bytes 18874368 | tf_op jit(solution)/shard_map/all_to_all | solution.py:77
  788.3 36.1 %reshape.103 = bf16[49152,3,32]{2,1,0:T(4,128)(2,1)} reshape(bf16[16,2,147456]{2,1,0:T(2,128)(2,1)} %all-to-all-done) | data formatting | bytes 18874368
  824.3 58.5 %copy.231 = bf16[3,32,16,3072]{3,1,2,0:T(8,128)(2,1)} copy(bf16[3,32,16,3072]{1,0,3,2:T(4,128)(2,1)} %bitcast.129) | data formatting | bytes 18874368 | tf_op jit(solution)/shard_map/all_to_all | solution.py:78
  892.0 11.9 bitcast_convert_fusion
  903.9 13.1 fusion.10
  917.0 20.5 %convolution_bitcast_fusion.1 = f32[3,1024,3072]{2,1,0:T(8,128)} fusion(bf16[3,512,3072]{2,1,0:T(8,128)(2,1)} %bitcast.143, bf16[512,512]{1,0:T(8,128)(2,1)S(1)} %copy-done.13, bf16[512,512]{1,0:T(8,128)(2,1)S(1)} %copy-done), kind=kOutput, calls=%fused_computation.27 | convolution fusion | flops 9665773568 | bytes 48234496 | tf_op jit(solution)/shard_map/wy,cyp->cwp/dot_general | solution.py:27
  937.5 16.8 %fusion.5 = bf16[3,512,3072]{2,1,0:T(8,128)(2,1)S(1)} fusion(f32[3,1024,3072]{2,1,0:T(8,128)} %convolution_bitcast_fusion.1, f32[512,3072]{1,0:T(8,128)} %fusion.10, f32[3]{0:T(128)S(1)} %copy-done.12, f32[512,3072]{1,0:T(8,128)} %bitcast.144), kind=kLoop, calls=%fused_computation.9 | loop fusion | flops 23592960 | bytes 59768844 | tf_op jit(solution)/shard_map/convert_element_type | solution.py:85
  954.4 39.2 %copy.203 = bf16[3,512,3072]{2,0,1:T(4,128)(2,1)} copy(bf16[3,512,3072]{2,1,0:T(8,128)(2,1)S(1)} %fusion.5) | data formatting | bytes 18874368 | tf_op jit(solution)/shard_map/convert_element_type | solution.py:85
  1000.1 16.0 %fusion.32 = (f32[3,32,128,1,128]{2,4,3,1,0:T(8,128)}, f32[3,32,128,1,128]{2,4,3,1,0:T(8,128)}, f32[3,32,128,1,128]{2,4,3,1,0:T(8,128)}, f32[3,32,128,1,128]{2,4,3,1,0:T(8,128)}) fusion(f32[3,32,128,3,768]{2,4,3,1,0:T(8,128)} %convolution_bitcast_fusion), kind=kLoop, calls=%fused_computation.70 | loop fusion | bytes 50331648 | tf_op jit(solution)/shard_map/jit(_roll_static)/slice | solution.py:19
  1016.1 50.3 %fusion.7 = (f32[3,32,128,3,128]{2,4,3,1,0:T(8,128)}, f32[3,32,128,3,128]{2,4,3,1,0:T(8,128)}) fusion(f32[3,32,128,3,768]{2,4,3,1,0:T(8,128)} %convolution_bitcast_fusion, f32[3,32,128,2,128]{2,4,3,1,0:T(8,128)} %get-tuple-element.8, f32[3,32,128,1,128]{2,4,3,1,0:T(8,128)} %get-tuple-element.12, f32[3,32,128,1,128]{2,4,3,1,0:T(8,128)} %get-tuple-element.11, ...), kind=kLoop, calls=%fused_computation.13 | loop fusion | flops 37748736 | bytes 150994944 | tf_op jit(solution)/shard_map/add | solution.py:19
  1066.3 18.7 %copy.189 = f32[3,32,128,384]{3,2,1,0:T(8,128)} copy(f32[3,32,128,384]{2,3,1,0:T(8,128)} %bitcast.136) | data formatting | bytes 37748736 | tf_op jit(solution)/shard_map/reshape | solution.py:20
  1085.0 18.7 %copy.188 = f32[3,32,128,384]{3,2,1,0:T(8,128)} copy(f32[3,32,128,384]{2,3,1,0:T(8,128)} %bitcast.135) | data formatting | bytes 37748736 | tf_op jit(solution)/shard_map/reshape | solution.py:20
  1103.7 24.5 %fusion.25 = f32[3,32,128,3,384]{4,2,3,1,0:T(8,128)} fusion(bf16[3,32,128,3,128]{2,4,3,1,0:T(8,128)(2,1)} %bitcast.128, bf16[128,128]{0,1:T(8,128)(2,1)S(1)} %bitcast.155, bf16[128,128]{0,1:T(8,128)(2,1)S(1)} %bitcast.153, bf16[128,128]{0,1:T(8,128)(2,1)S(1)} %bitcast.151), kind=kOutput, calls=%fused_computation.49 | convolution fusion | flops 3624173568 | bytes 66158592 | tf_op jit(solution)/shard_map/dot_general | solution.py:12
  1128.2 9.1 fusion.34
  1137.3 14.4 %fusion.33 = (f32[3,32,128,2,128]{4,2,3,1,0:T(8,128)S(1)}, f32[3,32,128,2,128]{4,2,3,1,0:T(8,128)}) fusion(f32[3,32,128,3,384]{4,2,3,1,0:T(8,128)} %fusion.25), kind=kLoop, calls=%fused_computation.71 | loop fusion | bytes 50331648 | tf_op jit(solution)/shard_map/jit(_roll_static)/slice | solution.py:19
  1151.7 19.5 %fusion.6 = f32[3,32,128,3,128]{4,2,3,1,0:T(8,128)} fusion(f32[3,32,128,3,384]{4,2,3,1,0:T(8,128)} %fusion.25, f32[3,32,128,2,128]{4,2,3,1,0:T(8,128)} %get-tuple-element.16, f32[3,32,128,1,128]{4,2,3,1,0:T(8,128)} %get-tuple-element.18, f32[3,32,128,1,128]{4,2,3,1,0:T(8,128)S(1)} %get-tuple-element.17, f32[3,32,128,2,128]{4,2,3,1,0:T(8,128)S(1)} %get-tuple-element.15), kind=kLoop, calls=%fused_computation.11 | loop fusion | flops 18874368 | bytes 75497472 | tf_op jit(solution)/shard_map/add | solution.py:19
  1171.2 18.6 %copy.193 = f32[3,32,128,3,128]{2,4,3,1,0:T(8,128)} copy(f32[3,32,128,3,128]{4,2,3,1,0:T(8,128)} %fusion.6) | data formatting | bytes 37748736 | tf_op jit(solution)/shard_map/add | solution.py:19
  1189.8 13.1 fusion.11
  1221.6 11.6 convert_bitcast_fusion.1
  1233.2 15.7 %copy.213 = f32[3,2,16,128,384]{4,3,2,1,0:T(8,128)} copy(f32[3,2,16,128,384]{4,2,0,3,1:T(8,128)} %convert_bitcast_fusion.1) | data formatting | bytes 37748736 | tf_op jit(solution)/shard_map/convert_element_type | solution.py:104
  1249.9 33.5 %all_gather.3 = bf16[2,49152]{1,0:T(2,128)(2,1)S(1)} all-gather(bf16[2,3072]{1,0:T(2,128)(2,1)S(1)} %pad_maximum_fusion.3), channel_id=1, replica_groups=mesh['row'=16,'col'=2] {'row'}, dimensions={1}, use_global_device_ids=true | all-gather | bytes 208896 | tf_op jit(solution)/shard_map/all_gather | solution.py:87
  1288.2 8.9 convert_bitcast_fusion
  1297.1 13.2 copy.204
  1310.3 20.5 %reshape.90 = f32[3,32,128,384]{3,2,1,0:T(8,128)} reshape(f32[3,32,16,3072]{3,2,1,0:T(8,128)} %copy.204) | data formatting | bytes 37748736 | tf_op jit(solution)/shard_map/convert_element_type | solution.py:104
  1330.8 34.6 %add_convert_fusion = bf16[3,32,128,384]{3,2,1,0:T(8,128)(2,1)} fusion(f32[3,32,128,384]{3,2,1,0:T(8,128)} %copy.189, f32[3,32,128,384]{3,2,1,0:T(8,128)} %copy.188, f32[3,32,128,384]{3,2,1,0:T(8,128)} %reshape.90, f32[3,32,128,384]{3,2,1,0:T(8,128)} %bitcast.137, f32[32,128,384]{2,1,0:T(8,128)} %multiply_add_fusion, f32[32,128,384]{2,1,0:T(8,128)} %copy.194, ...), kind=kLoop, calls=%fused_computation.24 | loop fusion | flops 51904512 | bytes 103809040 | tf_op jit(solution)/shard_map/convert_element_type | solution.py:113
  (87 shorter events, 77.2 us)
Async XLA Ops:
  9.1 109.4 %all-to-all-start.3 = ((bf16[3,32,128,384]{3,2,0,1:T(8,128)(2,1)}), bf16[3,32,128,384]{3,2,0,1:T(8,128)(2,1)}, u32[]{:S(2)}, u32[]{:S(2)}) async-start(bf16[3,32,128,384]{3,2,0,1:T(8,128)(2,1)} %copy.205), calls=%async_computation.3 | async-start | bytes 18874368 | tf_op jit(solution)/shard_map/all_to_all | solution.py:95
  118.5 125.8 %all-to-all-start.4 = ((bf16[3,32,128,384]{2,3,0,1:T(8,128)(2,1)}), bf16[3,32,128,384]{2,3,0,1:T(8,128)(2,1)}, u32[]{:S(2)}, u32[]{:S(2)}) async-start(bf16[3,32,128,384]{2,3,0,1:T(8,128)(2,1)} %copy.207), calls=%async_computation.4 | async-start | bytes 18874368 | tf_op jit(solution)/shard_map/all_to_all | solution.py:94
  244.3 210.4 %all-to-all-start.1 = ((bf16[16,2,147456]{2,1,0:T(2,128)(2,1)}), bf16[16,2,147456]{2,1,0:T(2,128)(2,1)}, u32[]{:S(2)}, u32[]{:S(2)}) async-start(bf16[16,2,147456]{2,1,0:T(2,128)(2,1)} %reshape.104), calls=%async_computation.1 | async-start | bytes 18874368 | tf_op jit(solution)/shard_map/all_to_all | solution.py:77
  454.7 326.3 %all-to-all-start = ((bf16[16,2,147456]{2,1,0:T(2,128)(2,1)}), bf16[16,2,147456]{2,1,0:T(2,128)(2,1)}, u32[]{:S(2)}, u32[]{:S(2)}) async-start(bf16[16,2,147456]{2,1,0:T(2,128)(2,1)} %reshape.102), calls=%async_computation | async-start | bytes 18874368 | tf_op jit(solution)/shard_map/all_to_all | solution.py:78
  462.3 12.7 copy-start.9
  462.3 13.1 copy-start.10
  475.2 42.2 %copy-start.2 = (bf16[1,128,128]{1,2,0:T(8,128)(2,1)}, bf16[1,128,128]{1,2,0:T(8,128)(2,1)S(1)}, u32[]{:S(2)}) copy-start(bf16[1,128,128]{1,2,0:T(8,128)(2,1)S(1)} %copy.239) | copy-start | bytes 98308
  475.3 42.1 %copy-start.4 = (bf16[1,128,128]{1,2,0:T(8,128)(2,1)}, bf16[1,128,128]{1,2,0:T(8,128)(2,1)S(1)}, u32[]{:S(2)}) copy-start(bf16[1,128,128]{1,2,0:T(8,128)(2,1)S(1)} %copy.240) | copy-start | bytes 98308
  475.4 41.9 %copy-start.6 = (bf16[1,128,128]{1,2,0:T(8,128)(2,1)}, bf16[1,128,128]{1,2,0:T(8,128)(2,1)S(1)}, u32[]{:S(2)}) copy-start(bf16[1,128,128]{1,2,0:T(8,128)(2,1)S(1)} %copy.241) | copy-start | bytes 98308
  570.6 5.7 copy-start.1
  576.3 12.7 copy-start.8
  576.3 31.4 %slice-start.3 = ((s8[6291456]{0:T(1024)(128)(4,1)}), s8[2097152]{0:T(1024)(128)(4,1)S(1)}, s32[]{:S(2)}) async-start(s8[6291456]{0:T(1024)(128)(4,1)} %bitcast.145), calls=%async_computation.9 | async-start | bytes 4194304
  589.1 18.7 %slice-start.4 = ((s8[6291456]{0:T(1024)(128)(4,1)}), s8[4194304]{0:T(1024)(128)(4,1)S(1)}, s32[]{:S(2)}) async-start(s8[6291456]{0:T(1024)(128)(4,1)} %bitcast.145), calls=%async_computation.10 | async-start | bytes 8388608
  781.0 212.6 %all-to-all-start.5 = ((bf16[3,16,256,384]{3,1,0,2:T(8,128)(2,1)}), bf16[3,16,256,384]{3,1,0,2:T(8,128)(2,1)}, u32[]{:S(2)}, u32[]{:S(2)}) async-start(bf16[3,16,256,384]{3,1,0,2:T(8,128)(2,1)} %copy.212), calls=%async_computation.5 | async-start | bytes 18874368 | tf_op jit(solution)/shard_map/all_to_all | solution.py:103
  882.8 9.2 slice-start
  882.8 9.2 copy-start
  882.8 9.2 slice-start.1
  885.6 6.3 slice-start.2
  903.9 13.1 copy-start.13
  917.0 20.5 %copy-start.12 = (f32[3]{0:T(128)S(1)}, f32[3]{0:T(128)}, u32[]{:S(2)}) copy-start(f32[3]{0:T(128)} %compare_convert_fusion.1) | copy-start | bytes 40
  993.6 294.6 %all-to-all-start.2 = ((bf16[3,512,3072]{2,0,1:T(4,128)(2,1)}), bf16[3,512,3072]{2,0,1:T(4,128)(2,1)}, u32[]{:S(2)}, u32[]{:S(2)}) async-start(bf16[3,512,3072]{2,0,1:T(4,128)(2,1)} %copy.203), calls=%async_computation.2 | async-start | bytes 25165824 | tf_op jit(solution)/shard_map/all_to_all | solution.py:90
  1085.0 18.7 %copy-start.3 = (bf16[1,128,128]{1,2,0:T(8,128)(2,1)S(1)}, bf16[1,128,128]{1,2,0:T(8,128)(2,1)}, u32[]{:S(2)}) copy-start(bf16[1,128,128]{1,2,0:T(8,128)(2,1)} %copy-done.2) | copy-start | bytes 98308
  1085.0 18.7 %copy-start.5 = (bf16[1,128,128]{1,2,0:T(8,128)(2,1)S(1)}, bf16[1,128,128]{1,2,0:T(8,128)(2,1)}, u32[]{:S(2)}) copy-start(bf16[1,128,128]{1,2,0:T(8,128)(2,1)} %copy-done.4) | copy-start | bytes 98308
  1085.0 18.7 %copy-start.7 = (bf16[1,128,128]{1,2,0:T(8,128)(2,1)S(1)}, bf16[1,128,128]{1,2,0:T(8,128)(2,1)}, u32[]{:S(2)}) copy-start(bf16[1,128,128]{1,2,0:T(8,128)(2,1)} %copy-done.6) | copy-start | bytes 98308
  1209.7 11.9 copy-start.11
where the time goes:
time: 1380 us; the launch traced here: 1370 us
  local copies, waits for them, and re-layouts  768 us (56%)
  other arithmetic  215 us (16%)
  waiting for transfers between devices  173 us (13%)
  matrix products  130 us (9%)
  starting transfers between devices  45.1 us (3%)
  blocking collectives  33.5 us (2%)
    unnamed x58, local copies, waits for them, and re-layouts  241 us
    all_to_all x1, waiting for transfers between devices, per_device(): lax.all_to_all(flat_speed, 'row', split_axis=2, concat_axis=1, tiled=True)  118 us
    all_to_all x2, local copies, waits for them, and re-layouts, per_device(): lax.all_to_all(flat_speed, 'row', split_axis=2, concat_axis=1, tiled=True)  106 us
    reshape x1, local copies, waits for them, and re-layouts, per_device(): flat_speed = velocity.reshape(3, local_rows, local_planes * stream_cells)  81.2 us
    slice x6, local copies, waits for them, and re-layouts, along_stream(): jnp.roll(upper, -1, axis=-2)  71 us
    add x3, other arithmetic, along_stream(): jnp.roll(lower, 1, axis=-2) + middle + jnp.roll(upper, -1, axis=-2)  69.8 us
    dot_general x3, matrix products, along_stream(): product = jnp.dot(tiles, joined, preferred_element_type=jnp.float32)  65.7 us
    all_to_all x1, local copies, waits for them, and re-layouts, per_device(): lax.all_to_all(flat_adjoint, 'row', split_axis=2, concat_axis=1, tiled=True)  58.5 us
  transfers between devices with their start and end apart: 6, of which 2 were waited for; matrix products, arithmetic and copies ran while one was open for 75% of the time, Pallas kernels for 0%

commit v1 on v0

--- a/solution.py
+++ b/solution.py
@@ -74,7 +74,12 @@
     flat_speed = velocity.reshape(3, local_rows, local_planes * stream_cells)
     flat_adjoint = adjoint_velocity.reshape(3, local_rows, local_planes * stream_cells)
     speed_lines, adjoint_lines = (
-        lax.all_to_all(flat_speed, "row", split_axis=2, concat_axis=1, tiled=True),
+        jnp.concatenate(
+            lax.all_to_all(
+                jnp.stack(jnp.split(flat_speed, lax.axis_size("row"), axis=2)), "row", 0, 0
+            ),
+            axis=1,
+        ),
         lax.all_to_all(flat_adjoint, "row", split_axis=2, concat_axis=1, tiled=True),
     )
     normal_speed, normal_adjoint, normal_curve = normal_products(

time: 1380 us -> 1230 us (0.89)
  local copies, waits for them, and re-layouts: 768 us -> 571 us
  waiting for transfers between devices: 173 us -> 217 us
    all_to_all x1, waiting for transfers between devices: 0.01 us -> 146 us  [per_device(): lax.all_to_all(flat_adjoint, 'row', split_axis=2, concat_axis=1, tiled=True)]
    all_to_all x1, waiting for transfers between devices: 118 us -> 0.01 us  [per_device(): lax.all_to_all(jnp.stack(jnp.split(flat_speed, lax.axis_size('row'), axis...]
    all_to_all x2 -> x0, local copies, waits for them, and re-layouts: 106 us -> none  [per_device(): lax.all_to_all(flat_speed, 'row', split_axis=2, concat_axis=1, tiled=True)]
    reshape x1, local copies, waits for them, and re-layouts: 81.2 us -> 13.1 us  [per_device(): flat_speed = velocity.reshape(3, local_rows, local_planes * stream_cells)]
    unnamed x58 -> x71, local copies, waits for them, and re-layouts: 241 us -> 197 us
    all_to_all x1, waiting for transfers between devices: 0.01 us -> 16.1 us  [per_device(): lax.all_to_all(velocity, 'col', split_axis=1, concat_axis=2, tiled=True)]
  transfers between devices with their start and end apart: 6 -> 6, of which waited for: 2 -> 3; matrix products, arithmetic and copies ran while one was open for 75% -> 68% of each run, Pallas kernels for 0% -> 0%
where the time goes in v1:
time: 1230 us; the launch traced here: 1220 us
  local copies, waits for them, and re-layouts  571 us (46%)
  waiting for transfers between devices  217 us (18%)
  other arithmetic  214 us (17%)
  matrix products  133 us (11%)
  starting transfers between devices  46.7 us (4%)
  blocking collectives  33.5 us (3%)
    unnamed x71, local copies, waits for them, and re-layouts  197 us
    all_to_all x1, waiting for transfers between devices, per_device(): lax.all_to_all(flat_adjoint, 'row', split_axis=2, concat_axis=1, tiled=True)  146 us
    slice x6, local copies, waits for them, and re-layouts, along_stream(): jnp.roll(upper, -1, axis=-2)  71 us
    add x3, other arithmetic, along_stream(): jnp.roll(lower, 1, axis=-2) + middle + jnp.roll(upper, -1, axis=-2)  69.8 us
    dot_general x3, matrix products, along_stream(): product = jnp.dot(tiles, joined, preferred_element_type=jnp.float32)  65.7 us
    all_to_all x1, local copies, waits for them, and re-layouts, per_device(): lax.all_to_all(flat_adjoint, 'row', split_axis=2, concat_axis=1, tiled=True)  58.5 us
    all_to_all x1, waiting for transfers between devices, per_device(): lax.all_to_all(adjoint_velocity, 'col', split_axis=1, concat_axis=2, tile...  55 us
    convert_element_type x1, local copies, waits for them, and re-layouts, per_device(): normal_term = adjoint_terms(speed_lines, adjoint_lines, normal_speed, nor...  39.2 us
  transfers between devices with their start and end apart: 6, of which 3 were waited for; matrix products, arithmetic and copies ran while one was open for 68% of the time, Pallas kernels for 0%

profile of v1, /device:TPU:13, one launch (start us, length us, event | category | flops | bytes accessed | tf_op | source)
XLA Modules:
  0.0 1216.8 jit_solution(10696782658706508443)
XLA Ops:
  0.0 9.1 copy.224
  16.6 12.6 %copy.208 = bf16[3,32,128,384]{2,3,1,0:T(8,128)(2,1)} copy(bf16[3,32,128,384]{3,2,1,0:T(8,128)(2,1)} %param.12) | data formatting | bytes 18874368 | tf_op args[1]
  29.2 12.6 %copy.207 = bf16[3,32,128,384]{2,3,1,0:T(8,128)(2,1)} copy(bf16[3,32,128,384]{3,2,1,0:T(8,128)(2,1)} %param.11) | data formatting | bytes 18874368 | tf_op args[0]
  42.5 12.5 %add_convert_fusion.2 = bf16[3,32,128,384]{2,3,1,0:T(8,128)(2,1)} fusion(bf16[3,32,128,384]{2,3,1,0:T(8,128)(2,1)} %copy.208, bf16[3,32,128,384]{2,3,1,0:T(8,128)(2,1)} %copy.207, f32[]{:T(128)} %bitcast.187), kind=kLoop, calls=%fused_computation.26 | loop fusion | flops 23592960 | bytes 28311556 | tf_op jit(solution)/shard_map/convert_element_type | solution.py:65
  55.0 8.5 copy.226
  63.5 55.0 %all-to-all-done.3 = bf16[3,32,128,384]{3,2,0,1:T(8,128)(2,1)} async-done(((bf16[3,32,128,384]{3,2,0,1:T(8,128)(2,1)}), bf16[3,32,128,384]{3,2,0,1:T(8,128)(2,1)}, u32[]{:S(2)}, u32[]{:S(2)}) %all-to-all-start.3) | async-done | bytes 9437216 | tf_op jit(solution)/shard_map/all_to_all | solution.py:100
  118.5 8.5 all-to-all-start.4
  127.0 48.7 %copy.217 = bf16[3,32,128,384]{1,0,3,2:T(4,128)(2,1)} copy(bf16[3,32,128,384]{3,2,1,0:T(8,128)(2,1)} %param.13) | data formatting | bytes 18874368 | tf_op args[2]
  175.7 36.1 %reshape.110 = bf16[16,2,147456]{2,1,0:T(2,128)(2,1)} reshape(bf16[49152,3,32]{2,1,0:T(4,128)(2,1)} %bitcast.190) | data formatting | bytes 18874368
  211.7 16.1 %all-to-all-done.4 = bf16[3,32,128,384]{2,3,0,1:T(8,128)(2,1)} async-done(((bf16[3,32,128,384]{2,3,0,1:T(8,128)(2,1)}), bf16[3,32,128,384]{2,3,0,1:T(8,128)(2,1)}, u32[]{:S(2)}, u32[]{:S(2)}) %all-to-all-start.4) | async-done | bytes 9437216 | tf_op jit(solution)/shard_map/all_to_all | solution.py:99
  236.0 12.7 %copy.220 = bf16[3,32,128,384]{3,2,1,0:T(8,128)(2,1)} copy(bf16[3,32,128,384]{2,3,1,0:T(8,128)(2,1)} %add_convert_fusion.2) | data formatting | bytes 18874368 | tf_op jit(solution)/shard_map/convert_element_type | solution.py:65
  248.7 13.1 %reshape.93 = bf16[3,32,49152]{2,1,0:T(8,128)(2,1)} reshape(bf16[3,32,128,384]{3,2,1,0:T(8,128)(2,1)} %copy.220) | data formatting | bytes 18874368 | tf_op jit(solution)/shard_map/reshape | solution.py:74
  292.7 145.9 %all-to-all-done = bf16[16,2,147456]{2,1,0:T(2,128)(2,1)} async-done(((bf16[16,2,147456]{2,1,0:T(2,128)(2,1)}), bf16[16,2,147456]{2,1,0:T(2,128)(2,1)}, u32[]{:S(2)}, u32[]{:S(2)}) %all-to-all-start) | async-done | bytes 9437216 | tf_op jit(solution)/shard_map/all_to_all | solution.py:83
  446.1 12.7 %copy.205 = bf16[3,32,128,384]{2,3,1,0:T(8,128)(2,1)} copy(bf16[3,32,128,384]{3,2,1,0:T(8,128)(2,1)} %param.13) | data formatting | bytes 18874368 | tf_op args[2]
  460.1 40.9 %convolution_bitcast_fusion = f32[3,32,128,3,768]{2,4,3,1,0:T(8,128)} fusion(bf16[3,32,128,3,128]{2,4,3,1,0:T(8,128)(2,1)} %bitcast.191, bf16[128,768]{0,1:T(8,128)(2,1)S(1)} %constant_dynamic-update-slice_fusion), kind=kOutput, calls=%fused_computation | convolution fusion | flops 7247757312 | bytes 122880000 | tf_op jit(solution)/shard_map/dot_general | solution.py:12
  501.1 31.5 %fusion.47 = (f32[3,32,128,2,128]{2,4,3,1,0:T(8,128)}, f32[3,32,128,2,128]{2,4,3,1,0:T(8,128)}, f32[3,32,128,2,128]{2,4,3,1,0:T(8,128)}, f32[3,32,128,2,128]{2,4,3,1,0:T(8,128)}) fusion(f32[3,32,128,3,768]{2,4,3,1,0:T(8,128)} %convolution_bitcast_fusion), kind=kLoop, calls=%fused_computation.101 | loop fusion | bytes 100663296 | tf_op jit(solution)/shard_map/jit(_roll_static)/slice | solution.py:19
  532.6 9.1 copy.225
  541.7 12.6 %copy.228 = bf16[3,2,16,128,384]{4,3,1,2,0:T(8,128)(2,1)} copy(bf16[3,2,16,128,384]{3,4,0,2,1:T(8,128)(2,1)} %bitcast.54) | data formatting | bytes 18874368 | tf_op jit(solution)/shard_map/all_to_all | solution.py:99
  560.1 12.7 %fusion.9 = f32[16,256,384]{2,1,0:T(8,128)} fusion(bf16[3,16,256,384]{3,2,1,0:T(8,128)(2,1)} %bitcast.192, bf16[3,16,256,384]{3,2,1,0:T(8,128)(2,1)} %bitcast.198, bf16[256,256]{1,0:T(8,128)(2,1)S(1)} %copy-done.1), kind=kOutput, calls=%fused_computation.18 | convolution fusion | flops 2428502016 | bytes 25296896 | tf_op jit(solution)/shard_map/vz,cyzx->cyvx/dot_general | solution.py:33
  572.8 18.7 %convolution_bitcast_fusion.2 = f32[3,16,512,384]{3,2,1,0:T(8,128)} fusion(bf16[3,16,256,384]{3,2,1,0:T(8,128)(2,1)} %bitcast.193, bf16[256,256]{1,0:T(8,128)(2,1)S(1)} %copy-done.8, bf16[256,256]{1,0:T(8,128)(2,1)S(1)} %copy-done.1), kind=kOutput, calls=%fused_computation.28 | convolution fusion | flops 4832362496 | bytes 47448064 | tf_op jit(solution)/shard_map/vz,cyzx->cyvx/dot_general | solution.py:35
  591.5 19.2 %fusion.2 = bf16[3,16,256,384]{3,2,1,0:T(8,128)(2,1)} fusion(f32[3,16,512,384]{3,2,1,0:T(8,128)} %convolution_bitcast_fusion.2, f32[16,256,384]{2,1,0:T(8,128)} %fusion.9, f32[3]{0:T(128)S(1)} %compare_convert_fusion, f32[16,256,384]{2,1,0:T(8,128)S(1)} %bitcast.204), kind=kLoop, calls=%fused_computation.5 | loop fusion | flops 23592960 | bytes 59768844 | tf_op jit(solution)/shard_map/convert_element_type | solution.py:107
  610.7 12.8 %copy.231 = bf16[3,16,256,384]{3,1,0,2:T(8,128)(2,1)} copy(bf16[3,16,256,384]{3,2,1,0:T(8,128)(2,1)} %fusion.2) | data formatting | bytes 18874368 | tf_op jit(solution)/shard_map/convert_element_type | solution.py:107
  623.5 35.8 %reshape.111 = bf16[49152,3,32]{2,1,0:T(4,128)(2,1)} reshape(bf16[16,2,147456]{2,1,0:T(2,128)(2,1)} %all-to-all-done) | data formatting | bytes 18874368
  659.4 58.5 %copy.250 = bf16[3,32,16,3072]{3,1,2,0:T(8,128)(2,1)} copy(bf16[3,32,16,3072]{1,0,3,2:T(4,128)(2,1)} %bitcast.189) | data formatting | bytes 18874368 | tf_op jit(solution)/shard_map/all_to_all | solution.py:83
  717.8 8.9 all-to-all-start.5
  726.7 8.8 copy.221
  735.6 15.8 %bitcast_convert_fusion = (bf16[3,512,3072]{2,1,0:T(8,128)(2,1)}, f32[3,3072,512]{1,2,0:T(8,128)}) fusion(bf16[3,512,3072]{2,1,0:T(8,128)(2,1)} %bitcast.202, bf16[512,512]{1,0:T(8,128)(2,1)S(1)} %copy-done), kind=kOutput, calls=%fused_computation.19 | convolution fusion | flops 4836556800 | bytes 38273024 | tf_op jit(solution)/shard_map/wy,cyp->cwp/dot_general | solution.py:25
  751.4 11.2 fusion.10
  768.5 20.1 %convolution_bitcast_fusion.1 = f32[3,1024,3072]{2,1,0:T(8,128)} fusion(bf16[3,512,3072]{2,1,0:T(8,128)(2,1)} %bitcast.199, bf16[512,512]{1,0:T(8,128)(2,1)S(1)} %copy-done.13, bf16[512,512]{1,0:T(8,128)(2,1)S(1)} %copy-done), kind=kOutput, calls=%fused_computation.27 | convolution fusion | flops 9665773568 | bytes 48234496 | tf_op jit(solution)/shard_map/wy,cyp->cwp/dot_general | solution.py:27
  788.6 16.9 %fusion.5 = bf16[3,512,3072]{2,1,0:T(8,128)(2,1)S(1)} fusion(f32[3,1024,3072]{2,1,0:T(8,128)} %convolution_bitcast_fusion.1, f32[512,3072]{1,0:T(8,128)} %fusion.10, f32[3]{0:T(128)S(1)} %copy-done.12, f32[512,3072]{1,0:T(8,128)} %bitcast_convert_fusion.1), kind=kLoop, calls=%fused_computation.9 | loop fusion | flops 23592960 | bytes 59768844 | tf_op jit(solution)/shard_map/convert_element_type | solution.py:90
  805.5 39.2 %copy.222 = bf16[3,512,3072]{2,0,1:T(4,128)(2,1)} copy(bf16[3,512,3072]{2,1,0:T(8,128)(2,1)S(1)} %fusion.5) | data formatting | bytes 18874368 | tf_op jit(solution)/shard_map/convert_element_type | solution.py:90
  851.0 16.0 %fusion.48 = (f32[3,32,128,1,128]{2,4,3,1,0:T(8,128)}, f32[3,32,128,1,128]{2,4,3,1,0:T(8,128)}, f32[3,32,128,1,128]{2,4,3,1,0:T(8,128)}, f32[3,32,128,1,128]{2,4,3,1,0:T(8,128)}) fusion(f32[3,32,128,3,768]{2,4,3,1,0:T(8,128)} %convolution_bitcast_fusion), kind=kLoop, calls=%fused_computation.102 | loop fusion | bytes 50331648 | tf_op jit(solution)/shard_map/jit(_roll_static)/slice | solution.py:19
  867.0 50.3 %fusion.7 = (f32[3,32,128,3,128]{2,4,3,1,0:T(8,128)}, f32[3,32,128,3,128]{2,4,3,1,0:T(8,128)}) fusion(f32[3,32,128,3,768]{2,4,3,1,0:T(8,128)} %convolution_bitcast_fusion, f32[3,32,128,2,128]{2,4,3,1,0:T(8,128)} %get-tuple-element.8, f32[3,32,128,1,128]{2,4,3,1,0:T(8,128)} %get-tuple-element.12, f32[3,32,128,1,128]{2,4,3,1,0:T(8,128)} %get-tuple-element.11, ...), kind=kLoop, calls=%fused_computation.13 | loop fusion | flops 37748736 | bytes 150994944 | tf_op jit(solution)/shard_map/add | solution.py:19
  917.2 18.7 %copy.211 = f32[3,32,128,384]{3,2,1,0:T(8,128)} copy(f32[3,32,128,384]{2,3,1,0:T(8,128)} %bitcast.195) | data formatting | bytes 37748736 | tf_op jit(solution)/shard_map/reshape | solution.py:20
  935.9 18.7 %copy.210 = f32[3,32,128,384]{3,2,1,0:T(8,128)} copy(f32[3,32,128,384]{2,3,1,0:T(8,128)} %bitcast.194) | data formatting | bytes 37748736 | tf_op jit(solution)/shard_map/reshape | solution.py:20
  954.6 24.5 %fusion.41 = f32[3,32,128,3,384]{4,2,3,1,0:T(8,128)} fusion(bf16[3,32,128,3,128]{2,4,3,1,0:T(8,128)(2,1)} %bitcast.188, bf16[128,128]{0,1:T(8,128)(2,1)S(1)} %bitcast.212, bf16[128,128]{0,1:T(8,128)(2,1)S(1)} %bitcast.210, bf16[128,128]{0,1:T(8,128)(2,1)S(1)} %bitcast.208), kind=kOutput, calls=%fused_computation.81 | convolution fusion | flops 3624173568 | bytes 66158592 | tf_op jit(solution)/shard_map/dot_general | solution.py:12
  979.1 9.1 fusion.50
  988.2 14.4 %fusion.49 = (f32[3,32,128,2,128]{4,2,3,1,0:T(8,128)S(1)}, f32[3,32,128,2,128]{4,2,3,1,0:T(8,128)}) fusion(f32[3,32,128,3,384]{4,2,3,1,0:T(8,128)} %fusion.41), kind=kLoop, calls=%fused_computation.103 | loop fusion | bytes 50331648 | tf_op jit(solution)/shard_map/jit(_roll_static)/slice | solution.py:19
  1002.6 19.5 %fusion.6 = f32[3,32,128,3,128]{4,2,3,1,0:T(8,128)} fusion(f32[3,32,128,3,384]{4,2,3,1,0:T(8,128)} %fusion.41, f32[3,32,128,2,128]{4,2,3,1,0:T(8,128)} %get-tuple-element.16, f32[3,32,128,1,128]{4,2,3,1,0:T(8,128)} %get-tuple-element.18, f32[3,32,128,1,128]{4,2,3,1,0:T(8,128)S(1)} %get-tuple-element.17, f32[3,32,128,2,128]{4,2,3,1,0:T(8,128)S(1)} %get-tuple-element.15), kind=kLoop, calls=%fused_computation.11 | loop fusion | flops 18874368 | bytes 75497472 | tf_op jit(solution)/shard_map/add | solution.py:19
  1022.1 18.6 %copy.215 = f32[3,32,128,3,128]{2,4,3,1,0:T(8,128)} copy(f32[3,32,128,3,128]{4,2,3,1,0:T(8,128)} %fusion.6) | data formatting | bytes 37748736 | tf_op jit(solution)/shard_map/add | solution.py:19
  1040.7 13.1 %fusion.11 = f32[32,128,384]{1,2,0:T(8,128)} fusion(f32[3,32,128,3,128]{2,4,3,1,0:T(8,128)} %copy.215, bf16[3,32,128,384]{2,3,1,0:T(8,128)(2,1)} %copy.205), kind=kLoop, calls=%fused_computation.23 | loop fusion | flops 12582912 | bytes 34603008 | tf_op jit(solution)/shard_map/reduce_sum | solution.py:45
  1072.5 11.6 convert_bitcast_fusion.1
  1084.2 15.7 %copy.232 = f32[3,2,16,128,384]{4,3,2,1,0:T(8,128)} copy(f32[3,2,16,128,384]{4,2,0,3,1:T(8,128)} %convert_bitcast_fusion.1) | data formatting | bytes 37748736 | tf_op jit(solution)/shard_map/convert_element_type | solution.py:109
  1100.8 33.5 %all_gather.3 = bf16[2,49152]{1,0:T(2,128)(2,1)S(1)} all-gather(bf16[2,3072]{1,0:T(2,128)(2,1)S(1)} %pad_maximum_fusion.3), channel_id=1, replica_groups=mesh['row'=16,'col'=2] {'row'}, dimensions={1}, use_global_device_ids=true | all-gather | bytes 208896 | tf_op jit(solution)/shard_map/all_gather | solution.py:92
  1139.2 8.9 convert_bitcast_fusion
  1148.1 13.2 %copy.223 = f32[3,32,16,3072]{3,2,1,0:T(8,128)} copy(f32[3,32,16,3072]{3,0,1,2:T(4,128)S(1)} %convert_bitcast_fusion) | data formatting | bytes 37748736 | tf_op jit(solution)/shard_map/convert_element_type | solution.py:109
  1161.3 20.5 %reshape.98 = f32[3,32,128,384]{3,2,1,0:T(8,128)} reshape(f32[3,32,16,3072]{3,2,1,0:T(8,128)} %copy.223) | data formatting | bytes 37748736 | tf_op jit(solution)/shard_map/convert_element_type | solution.py:109
  1181.7 34.6 %add_convert_fusion = bf16[3,32,128,384]{3,2,1,0:T(8,128)(2,1)} fusion(f32[3,32,128,384]{3,2,1,0:T(8,128)} %copy.211, f32[3,32,128,384]{3,2,1,0:T(8,128)} %copy.210, f32[3,32,128,384]{3,2,1,0:T(8,128)} %reshape.98, f32[3,32,128,384]{3,2,1,0:T(8,128)} %bitcast.196, f32[32,128,384]{2,1,0:T(8,128)} %multiply_add_fusion, f32[32,128,384]{2,1,0:T(8,128)} %copy.216, ...), kind=kLoop, calls=%fused_computation.24 | loop fusion | flops 51904512 | bytes 103809040 | tf_op jit(solution)/shard_map/convert_element_type | solution.py:118
  (101 shorter events, 97.6 us)
Async XLA Ops:
  9.1 109.4 %all-to-all-start.3 = ((bf16[3,32,128,384]{3,2,0,1:T(8,128)(2,1)}), bf16[3,32,128,384]{3,2,0,1:T(8,128)(2,1)}, u32[]{:S(2)}, u32[]{:S(2)}) async-start(bf16[3,32,128,384]{3,2,0,1:T(8,128)(2,1)} %copy.224), calls=%async_computation.3 | async-start | bytes 18874368 | tf_op jit(solution)/shard_map/all_to_all | solution.py:100
  118.5 109.4 %all-to-all-start.4 = ((bf16[3,32,128,384]{2,3,0,1:T(8,128)(2,1)}), bf16[3,32,128,384]{2,3,0,1:T(8,128)(2,1)}, u32[]{:S(2)}, u32[]{:S(2)}) async-start(bf16[3,32,128,384]{2,3,0,1:T(8,128)(2,1)} %copy.226), calls=%async_computation.4 | async-start | bytes 18874368 | tf_op jit(solution)/shard_map/all_to_all | solution.py:99
  227.9 210.8 %all-to-all-start = ((bf16[16,2,147456]{2,1,0:T(2,128)(2,1)}), bf16[16,2,147456]{2,1,0:T(2,128)(2,1)}, u32[]{:S(2)}, u32[]{:S(2)}) async-start(bf16[16,2,147456]{2,1,0:T(2,128)(2,1)} %reshape.110), calls=%async_computation | async-start | bytes 18874368 | tf_op jit(solution)/shard_map/all_to_all | solution.py:83
  438.6 279.2 %all-to-all-start.1 = ((bf16[16,3,32,3072]{3,2,1,0:T(8,128)(2,1)}), bf16[16,3,32,3072]{3,2,1,0:T(8,128)(2,1)}, u32[]{:S(2)}, u32[]{:S(2)}) async-start(bf16[16,3,32,3072]{3,2,1,0:T(8,128)(2,1)} %fusion.15), calls=%async_computation.1 | async-start | bytes 18874368 | tf_op jit(solution)/shard_map/all_to_all | solution.py:78
  446.1 12.7 %copy-start.9 = (bf16[3,128,128]{2,1,0:T(8,128)(2,1)S(1)}, bf16[3,128,128]{2,1,0:T(8,128)(2,1)}, u32[]{:S(2)}) copy-start(bf16[3,128,128]{2,1,0:T(8,128)(2,1)} %param.15) | copy-start | bytes 294916
  446.1 13.1 %copy-start.10 = (bf16[3,128,128]{2,1,0:T(8,128)(2,1)S(1)}, bf16[3,128,128]{2,1,0:T(8,128)(2,1)}, u32[]{:S(2)}) copy-start(bf16[3,128,128]{2,1,0:T(8,128)(2,1)} %param.16) | copy-start | bytes 294916
  458.9 42.2 %copy-start.2 = (bf16[1,128,128]{1,2,0:T(8,128)(2,1)}, bf16[1,128,128]{1,2,0:T(8,128)(2,1)S(1)}, u32[]{:S(2)}) copy-start(bf16[1,128,128]{1,2,0:T(8,128)(2,1)S(1)} %copy.254) | copy-start | bytes 98308
  459.0 42.1 %copy-start.4 = (bf16[1,128,128]{1,2,0:T(8,128)(2,1)}, bf16[1,128,128]{1,2,0:T(8,128)(2,1)S(1)}, u32[]{:S(2)}) copy-start(bf16[1,128,128]{1,2,0:T(8,128)(2,1)S(1)} %copy.255) | copy-start | bytes 98308
  459.1 41.9 %copy-start.6 = (bf16[1,128,128]{1,2,0:T(8,128)(2,1)}, bf16[1,128,128]{1,2,0:T(8,128)(2,1)S(1)}, u32[]{:S(2)}) copy-start(bf16[1,128,128]{1,2,0:T(8,128)(2,1)S(1)} %copy.256) | copy-start | bytes 98308
  554.3 5.7 copy-start.1
  560.1 12.7 %copy-start.8 = (bf16[256,256]{1,0:T(8,128)(2,1)S(1)}, bf16[256,256]{1,0:T(8,128)(2,1)}, u32[]{:S(2)}) copy-start(bf16[256,256]{1,0:T(8,128)(2,1)} %param.20) | copy-start | bytes 393220
  560.1 31.4 %slice-start.3 = ((s8[6291456]{0:T(1024)(128)(4,1)}), s8[2097152]{0:T(1024)(128)(4,1)S(1)}, s32[]{:S(2)}) async-start(s8[6291456]{0:T(1024)(128)(4,1)} %bitcast.203), calls=%async_computation.9 | async-start | bytes 4194304
  572.8 18.7 %slice-start.4 = ((s8[6291456]{0:T(1024)(128)(4,1)}), s8[4194304]{0:T(1024)(128)(4,1)S(1)}, s32[]{:S(2)}) async-start(s8[6291456]{0:T(1024)(128)(4,1)} %bitcast.203), calls=%async_computation.10 | async-start | bytes 8388608
  717.8 126.9 %all-to-all-start.5 = ((bf16[3,16,256,384]{3,1,0,2:T(8,128)(2,1)}), bf16[3,16,256,384]{3,1,0,2:T(8,128)(2,1)}, u32[]{:S(2)}, u32[]{:S(2)}) async-start(bf16[3,16,256,384]{3,1,0,2:T(8,128)(2,1)} %copy.231), calls=%async_computation.5 | async-start | bytes 18874368 | tf_op jit(solution)/shard_map/all_to_all | solution.py:108
  726.7 8.9 copy-start
  726.7 24.7 %slice-start = ((s8[9437184]{0:T(1024)(128)(4,1)}), s8[1048576]{0:T(1024)(128)(4,1)S(1)}, s32[]{:S(2)}) async-start(s8[9437184]{0:T(1024)(128)(4,1)} %bitcast.200), calls=%async_computation.6 | async-start | bytes 2097152
  735.6 15.8 %slice-start.1 = ((s8[9437184]{0:T(1024)(128)(4,1)}), s8[4194304]{0:T(1024)(128)(4,1)S(1)}, s32[]{:S(2)}) async-start(s8[9437184]{0:T(1024)(128)(4,1)} %bitcast.200), calls=%async_computation.7 | async-start | bytes 8388608
  735.6 15.8 %slice-start.2 = ((s8[9437184]{0:T(1024)(128)(4,1)}), s8[4194304]{0:T(1024)(128)(4,1)S(1)}, s32[]{:S(2)}) async-start(s8[9437184]{0:T(1024)(128)(4,1)} %bitcast.200), calls=%async_computation.8 | async-start | bytes 8388608
  762.6 5.9 copy-start.13
  768.5 20.1 %copy-start.12 = (f32[3]{0:T(128)S(1)}, f32[3]{0:T(128)}, u32[]{:S(2)}) copy-start(f32[3]{0:T(128)} %compare_convert_fusion.1) | copy-start | bytes 40
  844.7 294.5 %all-to-all-start.2 = ((bf16[3,512,3072]{2,0,1:T(4,128)(2,1)}), bf16[3,512,3072]{2,0,1:T(4,128)(2,1)}, u32[]{:S(2)}, u32[]{:S(2)}) async-start(bf16[3,512,3072]{2,0,1:T(4,128)(2,1)} %copy.222), calls=%async_computation.2 | async-start | bytes 25165824 | tf_op jit(solution)/shard_map/all_to_all | solution.py:95
  935.9 18.7 %copy-start.3 = (bf16[1,128,128]{1,2,0:T(8,128)(2,1)S(1)}, bf16[1,128,128]{1,2,0:T(8,128)(2,1)}, u32[]{:S(2)}) copy-start(bf16[1,128,128]{1,2,0:T(8,128)(2,1)} %copy-done.2) | copy-start | bytes 98308
  935.9 18.7 %copy-start.5 = (bf16[1,128,128]{1,2,0:T(8,128)(2,1)S(1)}, bf16[1,128,128]{1,2,0:T(8,128)(2,1)}, u32[]{:S(2)}) copy-start(bf16[1,128,128]{1,2,0:T(8,128)(2,1)} %copy-done.4) | copy-start | bytes 98308
  935.9 18.7 %copy-start.7 = (bf16[1,128,128]{1,2,0:T(8,128)(2,1)S(1)}, bf16[1,128,128]{1,2,0:T(8,128)(2,1)}, u32[]{:S(2)}) copy-start(bf16[1,128,128]{1,2,0:T(8,128)(2,1)} %copy-done.6) | copy-start | bytes 98308
  1060.6 11.9 copy-start.11
